TPU v7x, 128 devices: a whole 4x4x4 slice. The times are simulated.
128 devices in a mesh: col: 16 (over x, z_lo, core), row: 8 (over z_hi, y).
Axes of the slice: x: 4, y: 4, z: 4 (z_hi: 2, z_lo: 2; z = z_hi * 2 + z_lo), core: 2. Of those that a mesh axis runs over, the one named last changes fastest.
Arguments:
- features: bfloat16 [262144, 2048], P(('col', 'row')), may hold values from -6 to 6
- leaf_in: bfloat16 [262144, 128], P(('col', 'row')), may hold values from -0.1875 to 0.1875
- mix_in: bfloat16 [4, 256, 128, 256], P(None, ('col', 'row')), may hold values from -0.375 to 0.375
- mix_out: bfloat16 [4, 256, 128, 256], P(None, 'col'), may hold values from -0.375 to 0.375
- leaf_out: bfloat16 [262144, 128], P('col'), may hold values from -0.5 to 0.5
Outputs:
- result: bfloat16 [262144, 2048], P(('col', 'row'))
All inputs are finite; a program needn't handle non-finite values.
Results may differ from a plain program's by a relative error of at most 0.023.
Values may be sent and summed in bfloat16 or wider, within the bound.
A program may use at most 128 MiB of HBM per device.

v0:
```python
import jax
import jax.numpy as jnp
from jax import lax
from jax.sharding import PartitionSpec as P

LEAF_SIZE = 1024


def swapped(block, axis, stride):
    count = lax.axis_size(axis)
    route = []
    for low in range(count):
        high = low | 1 << stride
        if high != low and high < count:
            route += [(low, high), (high, low)]
    return lax.ppermute(block, axis, route)


def split_up(shard, dim, devices):
    before, after = (shard.shape[:dim], shard.shape[dim + 1 :])
    return jnp.moveaxis(shard.reshape(*before, devices, -1, *after), dim, 0)


def edges_of(length, count):
    unit = 8 if length >= 8 * count else 1
    return [length // unit * k // count * unit for k in range(1, count)]


def in_order(blocks, dim):
    blocks = jnp.moveaxis(blocks, 0, dim)
    lengths = blocks.shape
    return blocks.reshape(*lengths[:dim], lengths[dim] * lengths[dim + 1], *lengths[dim + 2 :])


def exchange_in_pieces(shard, axis, pieces, split_dim, concat_dim):
    blocks = split_up(shard, split_dim, lax.axis_size(axis))
    split_at = max(range(1, max(2, blocks.ndim - 1)), key=lambda d: blocks.shape[d])
    gathered = []
    for slab in jnp.split(blocks, edges_of(blocks.shape[split_at], pieces), axis=split_at):
        if slab.size:
            gathered.append(lax.all_to_all(slab, axis, split_axis=0, concat_axis=0, tiled=True))
    return in_order(jnp.concatenate(gathered, axis=split_at), concat_dim)


def partner_of(coeffs, level_bit):
    total_blocks = coeffs.shape[0]
    shaped = coeffs.reshape(
        (total_blocks // (2 << level_bit), 2, 1 << level_bit) + coeffs.shape[1:]
    )
    return jnp.flip(shaped, 1).reshape(coeffs.shape)


def forward_mix(weights, coeffs, partner):
    stacked = jnp.concatenate([coeffs, partner], axis=1)
    return jnp.einsum("bkj,bjr->bkr", weights, stacked, preferred_element_type=jnp.float32).astype(
        jnp.bfloat16
    )


def backward_terms(weights, gradient):
    rank_size = gradient.shape[1]
    direct = jnp.einsum(
        "bjk,bjr->bkr", weights[:, :, :rank_size], gradient, preferred_element_type=jnp.float32
    )
    crossed = jnp.einsum(
        "bjk,bjr->bkr", weights[:, :, rank_size:], gradient, preferred_element_type=jnp.float32
    )
    return (direct, crossed.astype(jnp.bfloat16))


def body(features, leaf_in, mix_in, mix_out, leaf_out):
    rank_size = leaf_in.shape[1]
    side_count = features.shape[1]
    blocks = features.shape[0] // LEAF_SIZE
    col_bits = lax.axis_size("col").bit_length() - 1
    row_bits = lax.axis_size("row").bit_length() - 1
    feature_blocks = features.reshape(blocks, LEAF_SIZE, side_count)
    leaf_rows = leaf_in.reshape(blocks, LEAF_SIZE, rank_size)
    coeffs = jnp.einsum(
        "bmk,bmr->bkr", leaf_rows, feature_blocks, preferred_element_type=jnp.float32
    ).astype(jnp.bfloat16)
    for level_bit in range(col_bits):
        partner = swapped(coeffs, "col", level_bit)
        coeffs = forward_mix(mix_in[level_bit], coeffs, partner)
    coeffs = exchange_in_pieces(coeffs, "row", 2, 2, 0)
    for level_bit in range(row_bits + 1):
        coeffs = forward_mix(mix_out[level_bit], coeffs, partner_of(coeffs, level_bit))
    out_rows = leaf_out.reshape(-1, LEAF_SIZE, rank_size)
    images = jnp.einsum(
        "bmk,bkr->bmr", out_rows, coeffs, preferred_element_type=jnp.float32
    ).astype(jnp.bfloat16)
    gradient = jnp.einsum(
        "bmk,bmr->bkr", out_rows, images, preferred_element_type=jnp.float32
    ).astype(jnp.bfloat16)
    for level_bit in reversed(range(row_bits + 1)):
        direct, crossed = backward_terms(mix_out[level_bit], gradient)
        gradient = (direct + partner_of(crossed, level_bit)).astype(jnp.bfloat16)
    gradient = lax.all_to_all(gradient, "row", split_axis=0, concat_axis=2, tiled=True)
    for level_bit in reversed(range(col_bits)):
        direct, crossed = backward_terms(mix_in[level_bit], gradient)
        gradient = (direct + swapped(crossed, "col", level_bit)).astype(jnp.bfloat16)
    result = jnp.einsum(
        "bmk,bkr->bmr", leaf_rows, gradient, preferred_element_type=jnp.float32
    ).astype(jnp.bfloat16)
    return result.reshape(features.shape)


def solution(mesh):
    in_specs = (
        P(("col", "row"), None),
        P(("col", "row"), None),
        P(None, ("col", "row"), None, None),
        P(None, "col", None, None),
        P("col", None),
    )
    out_specs = P(("col", "row"), None)
    return jax.shard_map(body, mesh=mesh, in_specs=in_specs, out_specs=out_specs, check_vma=False)
```

profile of v0, /device:TPU:24, one launch (start us, length us, event | category | flops | bytes accessed | tf_op | source)
XLA Modules:
  0.0 241.0 jit_solution(4041051786475556230)
XLA Ops:
  0.0 0.0 copy-start
  0.0 1.0 copy-done
  1.0 4.8 %convolution_convert_fusion.9 = bf16[2,128,2048]{2,1,0:T(8,128)(2,1)S(1)} fusion(bf16[2,1024,128]{2,1,0:T(8,128)(2,1)S(1)} %bitcast.138, bf16[2,1024,2048]{2,1,0:T(8,128)(2,1)} %bitcast.140), kind=kOutput, calls=%fused_computation.20 | convolution fusion | flops 1074266112 | bytes 9961472 | tf_op jit(solution)/shard_map/bmk,bmr->bkr/dot_general | solution.py:79
  5.8 0.1 collective-permute-start
  5.9 2.6 %collective-permute-done = bf16[2,128,2048]{2,1,0:T(8,128)(2,1)S(1)} collective-permute-done((bf16[2,128,2048]{2,1,0:T(8,128)(2,1)S(1)}, bf16[2,128,2048]{2,1,0:T(8,128)(2,1)S(1)}, u32[]{:S(2)}, u32[]{:S(2)}) %collective-permute-start) | collective-permute-done | bytes 1048608 | tf_op jit(solution)/shard_map/ppermute | solution.py:16
  8.5 0.0 copy-done.4
  8.5 0.5 fusion.12
  9.0 2.0 collective-permute-start.1
  11.0 23.5 %collective-permute-done.1 = bf16[2,128,2048]{2,1,0:T(8,128)(2,1)S(1)} collective-permute-done((bf16[2,128,2048]{2,1,0:T(8,128)(2,1)S(1)}, bf16[2,128,2048]{2,1,0:T(8,128)(2,1)S(1)}, u32[]{:S(2)}, u32[]{:S(2)}) %collective-permute-start.1) | collective-permute-done | bytes 1048608 | tf_op jit(solution)/shard_map/ppermute | solution.py:16
  34.5 0.4 fusion.13
  34.9 1.6 collective-permute-start.2
  36.5 23.1 %collective-permute-done.2 = bf16[2,128,2048]{2,1,0:T(8,128)(2,1)S(1)} collective-permute-done((bf16[2,128,2048]{2,1,0:T(8,128)(2,1)S(1)}, bf16[2,128,2048]{2,1,0:T(8,128)(2,1)S(1)}, u32[]{:S(2)}, u32[]{:S(2)}) %collective-permute-start.2) | collective-permute-done | bytes 1048608 | tf_op jit(solution)/shard_map/ppermute | solution.py:16
  59.6 0.5 fusion.14
  60.0 3.1 %collective-permute-start.3 = (bf16[2,128,2048]{2,1,0:T(8,128)(2,1)S(1)}, bf16[2,128,2048]{2,1,0:T(8,128)(2,1)S(1)}, u32[]{:S(2)}, u32[]{:S(2)}) collective-permute-start(bf16[2,128,2048]{2,1,0:T(8,128)(2,1)S(1)} %fusion.14), channel_id=1, source_target_pairs={{0,64},{64,0},{8,72},{72,8},{16,80},{80,16},{24,88},{88,24},{32,96... | collective-permute-start | bytes 3145736 | tf_op jit(solution)/shard_map/ppermute | solution.py:16
  63.1 22.1 %collective-permute-done.3 = bf16[2,128,2048]{2,1,0:T(8,128)(2,1)S(1)} collective-permute-done((bf16[2,128,2048]{2,1,0:T(8,128)(2,1)S(1)}, bf16[2,128,2048]{2,1,0:T(8,128)(2,1)S(1)}, u32[]{:S(2)}, u32[]{:S(2)}) %collective-permute-start.3) | collective-permute-done | bytes 1048608 | tf_op jit(solution)/shard_map/ppermute | solution.py:16
  85.3 0.9 convolution_convert_fusion.4
  86.2 0.5 copy.13
  86.8 0.9 fusion.91
  87.6 15.3 %all_to_all.28 = bf16[8,2,64,256]{3,2,1,0:T(8,128)(2,1)S(1)} all-to-all(bf16[8,2,64,256]{3,2,1,0:T(8,128)(2,1)S(1)} %get-tuple-element.10), channel_id=1, replica_groups=mesh['col'=16,'row'=8] {'row'}, dimensions={0} | all-to-all | bytes 1048576 | tf_op jit(solution)/shard_map/all_to_all | solution.py:41
  102.9 5.5 %all-to-all-start.1 = ((bf16[8,2,64,256]{3,2,1,0:T(8,128)(2,1)}), bf16[8,2,64,256]{3,2,1,0:T(8,128)(2,1)S(1)}, u32[]{:S(2)}, u32[]{:S(2)}) async-start(bf16[8,2,64,256]{3,2,1,0:T(8,128)(2,1)} %get-tuple-element.9), calls=%async_computation.1 | async-start | bytes 1048576 | tf_op jit(solution)/shard_map/all_to_all | solution.py:41
  108.4 4.3 %slice_bitcast_fusion.3 = (bf16[16,128,256]{2,1,0:T(8,128)(2,1)}, bf16[16,128,256]{2,1,0:T(8,128)(2,1)}, bf16[16,128,256]{2,1,0:T(8,128)(2,1)}, bf16[16,128,256]{2,1,0:T(8,128)(2,1)}) fusion(bf16[4,16,128,256]{3,2,1,0:T(8,128)(2,1)} %param.8), kind=kLoop, calls=%fused_computation.78 | loop fusion | bytes 8388608 | tf_op jit(solution)/shard_map/squeeze | solution.py:96
  112.7 3.6 %all-to-all-done.1 = bf16[8,2,64,256]{3,2,1,0:T(8,128)(2,1)S(1)} async-done(((bf16[8,2,64,256]{3,2,1,0:T(8,128)(2,1)}), bf16[8,2,64,256]{3,2,1,0:T(8,128)(2,1)S(1)}, u32[]{:S(2)}, u32[]{:S(2)}) %all-to-all-start.1) | async-done | bytes 524320 | tf_op jit(solution)/shard_map/all_to_all | solution.py:41
  116.4 1.0 reverse.3
  117.4 2.0 fusion.56
  119.4 1.0 rev.26
  120.5 2.0 fusion.53
  122.4 1.0 rev.27
  123.5 2.0 fusion.50
  125.5 0.1 rev.28
  125.6 3.0 %fusion.47 = bf16[16,256,128]{2,1,0:T(8,128)(2,1)} fusion(bf16[16,128,256]{2,1,0:T(8,128)(2,1)S(1)} %bitcast.164, bf16[16,128,256]{2,1,0:T(8,128)(2,1)S(1)} %bitcast.159, bf16[4,16,128,256]{3,2,1,0:T(8,128)(2,1)} %param.8), kind=kOutput, calls=%fused_computation.66 | convolution fusion | flops 273154048 | bytes 4194304 | tf_op jit(solution)/shard_map/bkj,bjr->bkr/dot_general | solution.py:55
  128.5 8.3 %fusion.59 = bf16[16,256,128]{2,1,0:T(8,128)(2,1)S(1)} fusion(bf16[16,1024,128]{2,1,0:T(8,128)(2,1)} %bitcast.165, bf16[16,256,128]{2,1,0:T(8,128)(2,1)} %fusion.47), kind=kOutput, calls=%fused_computation.74 | convolution fusion | flops 2152202240 | bytes 6291456 | tf_op jit(solution)/shard_map/bmk,bmr->bkr/dot_general | solution.py:92
  136.9 1.5 convolution_convert_fusion.13
  138.3 1.0 rev.29
  139.4 1.9 fusion.46
  141.3 0.0 copy-done.3
  141.3 0.4 convolution_convert_fusion.12
  141.7 1.0 rev.30
  142.8 1.9 fusion.45
  144.7 0.0 copy-done.2
  144.7 0.4 convolution_convert_fusion.11
  145.1 1.0 rev.31
  146.1 1.9 fusion.44
  148.1 1.4 convolution_convert_fusion.10
  149.4 1.3 rev.32
  150.8 2.4 %fusion.43 = bf16[16,128,256]{1,2,0:T(8,128)(2,1)} fusion(bf16[16,128,256]{1,2,0:T(8,128)(2,1)S(1)} %bitcast.146, bf16[16,128,256]{1,2,0:T(8,128)(2,1)S(1)} %fusion.44, bf16[16,128,256]{2,1,0:T(8,128)(2,1)} %get-tuple-element.5), kind=kOutput, calls=%fused_computation.57 | convolution fusion | flops 135790592 | bytes 3670016 | tf_op jit(solution)/shard_map/bjk,bjr->bkr/dot_general | solution.py:62
  153.2 5.8 %all-to-all-start.2 = ((bf16[16,128,256]{1,2,0:T(8,128)(2,1)}), bf16[16,128,256]{1,2,0:T(8,128)(2,1)S(1)}, u32[]{:S(2)}, u32[]{:S(2)}) async-start(bf16[16,128,256]{1,2,0:T(8,128)(2,1)} %fusion.43), calls=%async_computation.2 | async-start | bytes 2097152 | tf_op jit(solution)/shard_map/all_to_all | solution.py:98
  159.0 10.7 %all-to-all-done.2 = bf16[16,128,256]{1,2,0:T(8,128)(2,1)S(1)} async-done(((bf16[16,128,256]{1,2,0:T(8,128)(2,1)}), bf16[16,128,256]{1,2,0:T(8,128)(2,1)S(1)}, u32[]{:S(2)}, u32[]{:S(2)}) %all-to-all-start.2) | async-done | bytes 1048608 | tf_op jit(solution)/shard_map/all_to_all | solution.py:98
  169.7 0.1 copy.14
  169.8 0.4 fusion.8
  170.2 3.3 %collective-permute-start.4 = (bf16[2,128,2048]{1,2,0:T(8,128)(2,1)S(1)}, bf16[2,128,2048]{1,2,0:T(8,128)(2,1)S(1)}, u32[]{:S(2)}, u32[]{:S(2)}) collective-permute-start(bf16[2,128,2048]{1,2,0:T(8,128)(2,1)S(1)} %fusion.8), channel_id=1, source_target_pairs={{0,64},{64,0},{8,72},{72,8},{16,80},{80,16},{24,88},{88,24},{32,96... | collective-permute-start | bytes 3145736 | tf_op jit(solution)/shard_map/ppermute | solution.py:16
  173.5 19.9 %collective-permute-done.4 = bf16[2,128,2048]{1,2,0:T(8,128)(2,1)S(1)} collective-permute-done((bf16[2,128,2048]{1,2,0:T(8,128)(2,1)S(1)}, bf16[2,128,2048]{1,2,0:T(8,128)(2,1)S(1)}, u32[]{:S(2)}, u32[]{:S(2)}) %collective-permute-start.4) | collective-permute-done | bytes 1048608 | tf_op jit(solution)/shard_map/ppermute | solution.py:16
  193.4 0.4 add_convert_fusion.1
  193.8 0.4 fusion.9
  194.3 1.7 collective-permute-start.5
  196.0 17.4 %collective-permute-done.5 = bf16[2,128,2048]{1,2,0:T(8,128)(2,1)S(1)} collective-permute-done((bf16[2,128,2048]{1,2,0:T(8,128)(2,1)S(1)}, bf16[2,128,2048]{1,2,0:T(8,128)(2,1)S(1)}, u32[]{:S(2)}, u32[]{:S(2)}) %collective-permute-start.5) | collective-permute-done | bytes 1048608 | tf_op jit(solution)/shard_map/ppermute | solution.py:16
  213.4 0.4 fusion.7
  213.8 0.4 fusion.10
  214.2 1.2 collective-permute-start.6
  215.4 17.0 %collective-permute-done.6 = bf16[2,128,2048]{1,2,0:T(8,128)(2,1)S(1)} collective-permute-done((bf16[2,128,2048]{1,2,0:T(8,128)(2,1)S(1)}, bf16[2,128,2048]{1,2,0:T(8,128)(2,1)S(1)}, u32[]{:S(2)}, u32[]{:S(2)}) %collective-permute-start.6) | collective-permute-done | bytes 1048608 | tf_op jit(solution)/shard_map/ppermute | solution.py:16
  232.4 0.4 add_convert_fusion
  232.8 0.5 fusion.11
  233.3 0.1 collective-permute-start.7
  233.4 2.6 %collective-permute-done.7 = bf16[2,128,2048]{2,1,0:T(8,128)(2,1)S(1)} collective-permute-done((bf16[2,128,2048]{2,1,0:T(8,128)(2,1)S(1)}, bf16[2,128,2048]{2,1,0:T(8,128)(2,1)S(1)}, u32[]{:S(2)}, u32[]{:S(2)}) %collective-permute-start.7) | collective-permute-done | bytes 1048608 | tf_op jit(solution)/shard_map/ppermute | solution.py:16
  236.1 5.0 %convolution_convert_fusion = bf16[2,2048,1024]{1,2,0:T(8,128)(2,1)} fusion(bf16[2,1024,128]{2,1,0:T(8,128)(2,1)S(1)} %bitcast.139, bf16[2,128,2048]{1,2,0:T(8,128)(2,1)S(1)} %add_convert_fusion, bf16[2,128,2048]{2,1,0:T(8,128)(2,1)S(1)} %collective-permute-done.7, bf16[2,128,256]{2,1,0:T(8,128)(2,1)S(1)} %get-tuple-element.11), kind=kOutput, calls=%fused_computation.2 | convolution fusion | flops 1213726720 | bytes 11075584 | tf_op jit(solution)/shard_map/bmk,bkr->bmr/dot_general | solution.py:102
  (8 shorter events, 0.1 us)
Async XLA Ops:
  0.0 1.0 copy-start
  1.0 7.5 %copy-start.4 = (bf16[4,2,128,256]{3,2,1,0:T(8,128)(2,1)S(1)}, bf16[4,2,128,256]{3,2,1,0:T(8,128)(2,1)}, u32[]{:S(2)}) copy-start(bf16[4,2,128,256]{3,2,1,0:T(8,128)(2,1)} %param.7) | copy-start | bytes 1572868
  5.8 2.7 %collective-permute-start = (bf16[2,128,2048]{2,1,0:T(8,128)(2,1)S(1)}, bf16[2,128,2048]{2,1,0:T(8,128)(2,1)S(1)}, u32[]{:S(2)}, u32[]{:S(2)}) collective-permute-start(bf16[2,128,2048]{2,1,0:T(8,128)(2,1)S(1)} %convolution_convert_fusion.9), channel_id=1, source_target_pairs={{0,8},{8,0},{16,24},{24,16},{32,40},{40,32},{48,56},{56,48},{64,72... | collective-permute-start | bytes 3145736 | tf_op jit(solution)/shard_map/ppermute | solution.py:16
  9.0 25.5 %collective-permute-start.1 = (bf16[2,128,2048]{2,1,0:T(8,128)(2,1)S(1)}, bf16[2,128,2048]{2,1,0:T(8,128)(2,1)S(1)}, u32[]{:S(2)}, u32[]{:S(2)}) collective-permute-start(bf16[2,128,2048]{2,1,0:T(8,128)(2,1)S(1)} %fusion.12), channel_id=1, source_target_pairs={{0,16},{16,0},{8,24},{24,8},{32,48},{48,32},{40,56},{56,40},{64,80... | collective-permute-start | bytes 3145736 | tf_op jit(solution)/shard_map/ppermute | solution.py:16
  34.9 24.7 %collective-permute-start.2 = (bf16[2,128,2048]{2,1,0:T(8,128)(2,1)S(1)}, bf16[2,128,2048]{2,1,0:T(8,128)(2,1)S(1)}, u32[]{:S(2)}, u32[]{:S(2)}) collective-permute-start(bf16[2,128,2048]{2,1,0:T(8,128)(2,1)S(1)} %fusion.13), channel_id=1, source_target_pairs={{0,32},{32,0},{8,40},{40,8},{16,48},{48,16},{24,56},{56,24},{64,96... | collective-permute-start | bytes 3145736 | tf_op jit(solution)/shard_map/ppermute | solution.py:16
  60.0 25.2 %collective-permute-start.3 = (bf16[2,128,2048]{2,1,0:T(8,128)(2,1)S(1)}, bf16[2,128,2048]{2,1,0:T(8,128)(2,1)S(1)}, u32[]{:S(2)}, u32[]{:S(2)}) collective-permute-start(bf16[2,128,2048]{2,1,0:T(8,128)(2,1)S(1)} %fusion.14), channel_id=1, source_target_pairs={{0,64},{64,0},{8,72},{72,8},{16,80},{80,16},{24,88},{88,24},{32,96... | collective-permute-start | bytes 3145736 | tf_op jit(solution)/shard_map/ppermute | solution.py:16
  102.9 13.4 %all-to-all-start.1 = ((bf16[8,2,64,256]{3,2,1,0:T(8,128)(2,1)}), bf16[8,2,64,256]{3,2,1,0:T(8,128)(2,1)S(1)}, u32[]{:S(2)}, u32[]{:S(2)}) async-start(bf16[8,2,64,256]{3,2,1,0:T(8,128)(2,1)} %get-tuple-element.9), calls=%async_computation.1 | async-start | bytes 1048576 | tf_op jit(solution)/shard_map/all_to_all | solution.py:41
  139.4 1.9 copy-start.3
  142.8 1.9 copy-start.2
  146.1 1.9 copy-start.1
  153.2 16.5 %all-to-all-start.2 = ((bf16[16,128,256]{1,2,0:T(8,128)(2,1)}), bf16[16,128,256]{1,2,0:T(8,128)(2,1)S(1)}, u32[]{:S(2)}, u32[]{:S(2)}) async-start(bf16[16,128,256]{1,2,0:T(8,128)(2,1)} %fusion.43), calls=%async_computation.2 | async-start | bytes 2097152 | tf_op jit(solution)/shard_map/all_to_all | solution.py:98
  170.2 23.2 %collective-permute-start.4 = (bf16[2,128,2048]{1,2,0:T(8,128)(2,1)S(1)}, bf16[2,128,2048]{1,2,0:T(8,128)(2,1)S(1)}, u32[]{:S(2)}, u32[]{:S(2)}) collective-permute-start(bf16[2,128,2048]{1,2,0:T(8,128)(2,1)S(1)} %fusion.8), channel_id=1, source_target_pairs={{0,64},{64,0},{8,72},{72,8},{16,80},{80,16},{24,88},{88,24},{32,96... | collective-permute-start | bytes 3145736 | tf_op jit(solution)/shard_map/ppermute | solution.py:16
  194.3 19.1 %collective-permute-start.5 = (bf16[2,128,2048]{1,2,0:T(8,128)(2,1)S(1)}, bf16[2,128,2048]{1,2,0:T(8,128)(2,1)S(1)}, u32[]{:S(2)}, u32[]{:S(2)}) collective-permute-start(bf16[2,128,2048]{1,2,0:T(8,128)(2,1)S(1)} %fusion.9), channel_id=1, source_target_pairs={{0,32},{32,0},{8,40},{40,8},{16,48},{48,16},{24,56},{56,24},{64,96... | collective-permute-start | bytes 3145736 | tf_op jit(solution)/shard_map/ppermute | solution.py:16
  214.2 18.2 %collective-permute-start.6 = (bf16[2,128,2048]{1,2,0:T(8,128)(2,1)S(1)}, bf16[2,128,2048]{1,2,0:T(8,128)(2,1)S(1)}, u32[]{:S(2)}, u32[]{:S(2)}) collective-permute-start(bf16[2,128,2048]{1,2,0:T(8,128)(2,1)S(1)} %fusion.10), channel_id=1, source_target_pairs={{0,16},{16,0},{8,24},{24,8},{32,48},{48,32},{40,56},{56,40},{64,80... | collective-permute-start | bytes 3145736 | tf_op jit(solution)/shard_map/ppermute | solution.py:16
  233.3 2.7 %collective-permute-start.7 = (bf16[2,128,2048]{2,1,0:T(8,128)(2,1)S(1)}, bf16[2,128,2048]{2,1,0:T(8,128)(2,1)S(1)}, u32[]{:S(2)}, u32[]{:S(2)}) collective-permute-start(bf16[2,128,2048]{2,1,0:T(8,128)(2,1)S(1)} %fusion.11), channel_id=1, source_target_pairs={{0,8},{8,0},{16,24},{24,16},{32,40},{40,32},{48,56},{56,48},{64,72... | collective-permute-start | bytes 3145736 | tf_op jit(solution)/shard_map/ppermute | solution.py:16
where the time goes:
time: 245 us; the launch traced here: 241 us
  waiting for transfers between devices  143 us (58%)
  matrix products  44 us (18%)
  starting transfers between devices  24.4 us (10%)
  blocking collectives  15.3 us (6%)
  local copies, waits for them, and re-layouts  14.5 us (6%)
    ppermute x8, waiting for transfers between devices, swapped(): return lax.ppermute(block, axis, route)  128 us
    all_to_all x1, blocking collectives, exchange_in_pieces(): lax.all_to_all(slab, axis, split_axis=0, concat_axis=0, tiled=True)  15.3 us
    ppermute x8, starting transfers between devices, swapped(): return lax.ppermute(block, axis, route)  13 us
    dot_general x8, matrix products, forward_mix(): jnp.einsum('bkj,bjr->bkr', weights, stacked, preferred_element_type=jnp.f...  11.2 us
    all_to_all x1, waiting for transfers between devices, body(): lax.all_to_all(gradient, 'row', split_axis=0, concat_axis=2, tiled=True)  10.7 us
    dot_general x7, matrix products, backward_terms(): jnp.einsum('bjk,bjr->bkr', weights[:, :, :rank_size], gradient, preferred...  9.35 us
    dot_general x1, matrix products, body(): jnp.einsum('bmk,bmr->bkr', out_rows, images, preferred_element_type=jnp.f...  8.31 us
    rev x7, local copies, waits for them, and re-layouts, partner_of(): return jnp.flip(shaped, 1).reshape(coeffs.shape)  6.59 us
  transfers between devices with their start and end apart: 10, of which 10 were waited for; matrix products, arithmetic and copies ran while one was open for 2% of the time, Pallas kernels for 0%

commit v1 on v0

v1 whole, which is shorter than its diff:
```python
import jax
import jax.numpy as jnp
from jax import lax
from jax.experimental import pallas as pl
from jax.experimental.pallas import tpu as pltpu
from jax.sharding import PartitionSpec as P

LEAF = 1024
RANK = 128
LANES = 128
MESH = pl.DeviceIdType.MESH
F32 = jnp.float32
BF16 = jnp.bfloat16
LEVELS = 4


def pairs_of(bit):
    return [b for b in range(16) if not b >> bit & 1]


def pair_matrix(top, bottom):
    swapped = jnp.concatenate([bottom[:, RANK:], bottom[:, :RANK]], axis=1)
    return jnp.concatenate([top, swapped], axis=0)


def column(x, zl, k):
    return x * 4 + zl * 2 + k


def operator_kernel(
    features, leaf_in, mix_in, mix_out, leaf_out, returned,
    feat, basis, basis_t, win, win_t, wout, wout_t, lout, gram,
    coeffs, xa, xb, xr, home,
    load_sem, w_send, w_recv, w_local, sib_send, sib_recv, send_sem, recv_sem, out_sem,
):
    col, row = lax.axis_index("col"), lax.axis_index("row")
    x, zl, k = col // 4, col // 2 % 2, col % 2
    zh, y = row // 4, row % 4
    x_hi, x_lo, y_hi, y_lo = x // 2, x % 2, y // 2, y % 2
    right, left = (x + 1) % 4, (x + 3) % 4

    feat_loads = [
        pltpu.make_async_copy(
            features.at[:, pl.ds(j * 512, 512)], feat.at[j], load_sem.at[j]
        )
        for j in range(4)
    ]
    basis_load = pltpu.make_async_copy(leaf_in, basis, load_sem.at[4])
    wout_load = pltpu.make_async_copy(mix_out, wout, load_sem.at[5])
    lout_load = pltpu.make_async_copy(leaf_out, lout, load_sem.at[6])
    own_load = pltpu.make_async_copy(mix_in.at[:, zl], win.at[col], load_sem.at[7])
    basis_load.start()
    for load in feat_loads:
        load.start()
    own_load.start()
    lout_load.start()
    wout_load.start()

    def relative(m):
        px = (x + m + 1) % 4
        pz = (zl + m + m // 4) % 2
        pk = (k + m // 2 + m // 8) % 2
        return px, pz, pk

    def spread_row(m, q):
        px, pz, pk = relative(m)
        py = (x_lo + q + px) % 2 * 2 + (x_hi + pk) % 2
        return column(px, pz, pk), k * 4 + py

    def gather_row(m, q):
        px = (y_lo + k) % 2 * 2 + (y_hi + q + x) % 2
        return column(px, m % 2, zh), m // 2

    barrier = pltpu.get_barrier_semaphore()

    def greet(m, carry):
        px, pz, pk = relative(m)
        pl.semaphore_signal(
            barrier, device_id={"col": column(px, pz, pk), "row": row}, device_id_type=MESH
        )
        for q in range(2):
            for c, r in (spread_row(m, q), gather_row(m, q)):
                pl.semaphore_signal(
                    barrier, device_id={"col": c, "row": r}, device_id_type=MESH
                )
        return carry

    lax.fori_loop(0, 16, greet, 0)
    pl.semaphore_wait(barrier, 80)

    def ship(src, dst, send, recv, c, r):
        here = jnp.logical_and(c == col, r == row)

        @pl.when(here)
        def _():
            pltpu.make_async_copy(src, dst, recv).start()

        @pl.when(jnp.logical_not(here))
        def _():
            pltpu.make_async_remote_copy(
                src_ref=src, dst_ref=dst, send_sem=send, recv_sem=recv,
                device_id={"col": c, "row": r}, device_id_type=MESH,
            ).start()

    def weights_to(src, slot, n, recv, c):
        return pltpu.make_async_remote_copy(
            src_ref=src, dst_ref=win.at[slot], send_sem=w_send.at[n], recv_sem=recv,
            device_id={"col": c}, device_id_type=MESH,
        )

    def arrived(slot, sem):
        pltpu.make_async_copy(win.at[slot], win.at[slot], sem).wait()

    def to_sibling(src, slot, n):
        copy = pltpu.make_async_remote_copy(
            src_ref=src, dst_ref=win.at[slot], send_sem=sib_send.at[n], recv_sem=sib_recv.at[n],
            device_id={"col": column(x, zl, 1 - k)}, device_id_type=MESH,
        )
        copy.start()
        return copy

    mine = mix_in.at[:, zl]
    partner = column(x, 1 - zl, k)
    w1 = weights_to(mix_in.at[:, 1 - zl], col, 0, w_recv.at[0], partner)
    w2 = [
        weights_to(mine, col, 1, w_recv.at[1 + zl], column(right, zl, k)),
        weights_to(mine, col, 2, w_recv.at[3 + zl], column(left, zl, k)),
    ]
    w1.start()
    w2[0].start()
    w2[1].start()
    siblings = [to_sibling(mine, col, 0)]

    basis_load.wait()
    for leaf in range(2):
        basis_t[leaf] = basis[pl.ds(leaf * LEAF, LEAF), :].T

    def project(q):
        for j in range(2):
            feat_loads[2 * q + j].wait()
            for leaf in range(2):
                block = jnp.dot(
                    basis_t[leaf], feat[2 * q + j, pl.ds(leaf * LEAF, LEAF), :],
                    preferred_element_type=F32,
                ).astype(BF16)
                for i in range(4):
                    coeffs[q, 4 * j + i, leaf] = block[:, i * LANES : (i + 1) * LANES]

    def send_coeffs(q):
        def one(m, carry):
            px, pz, pk = relative(m)
            ship(
                coeffs.at[q, px * 2 + pk, pz], xa.at[q, col],
                send_sem.at[0, q, m], recv_sem.at[0, q], column(px, pz, pk), row,
            )
            return carry

        lax.fori_loop(0, 16, one, 0)

    project(0)
    send_coeffs(0)
    arrived(partner, w_recv.at[0])
    w2 += [
        weights_to(win.at[partner], partner, 3, w_recv.at[2 - zl], column(right, zl, k)),
        weights_to(win.at[partner], partner, 4, w_recv.at[4 - zl], column(left, zl, k)),
    ]
    w2[2].start()
    w2[3].start()
    siblings.append(to_sibling(win.at[partner], partner, 1))
    project(1)
    send_coeffs(1)

    from_left = [column(left, z, k) for z in range(2)]
    from_right = [column(right, z, k) for z in range(2)]
    arrived(from_right[0], w_recv.at[3])
    w3 = [weights_to(win.at[from_right[0]], from_right[0], 5, w_recv.at[5], column(left, zl, k))]
    w3[0].start()
    siblings.append(to_sibling(win.at[from_right[0]], from_right[0], 2))
    arrived(from_left[1], w_recv.at[2])
    w3.append(weights_to(win.at[from_left[1]], from_left[1], 6, w_recv.at[6], column(right, zl, k)))
    w3[1].start()
    siblings.append(to_sibling(win.at[from_left[1]], from_left[1], 3))
    arrived(from_left[0], w_recv.at[1])
    siblings.append(to_sibling(win.at[from_left[0]], from_left[0], 4))
    arrived(from_right[1], w_recv.at[4])
    siblings.append(to_sibling(win.at[from_right[1]], from_right[1], 5))

    lout_load.wait()

    def gram_of(i, carry):
        rows = lout[pl.ds(i * LEAF, LEAF), :]
        product = lax.dot_general(rows, rows, (((0,), (0,)), ((), ())), preferred_element_type=F32)
        high = product.astype(BF16)
        low = (product - high.astype(F32)).astype(BF16)
        gram[i] = jnp.concatenate([high, low], axis=1)
        return carry

    lax.fori_loop(0, 16, gram_of, 0)

    far = (x + 2) % 4
    for z in range(2):
        arrived(column(far, z, k), w_recv.at[5 + z])
        siblings.append(to_sibling(win.at[column(far, z, k)], column(far, z, k), 6 + z))

    wout_load.wait()

    for level in range(LEVELS):
        for n, b in enumerate(pairs_of(level)):
            wout_t[level, n] = pair_matrix(wout[level, b], wout[level, b | 1 << level]).T

    own_load.wait()
    for copy in siblings:
        copy.wait_recv()

    def received(buffer, phase, q):
        pltpu.make_async_copy(buffer.at[q], buffer.at[q], recv_sem.at[phase, q]).wait()

    def mix(buffer, q, level, matrix):
        for n, b in enumerate(pairs_of(level)):
            p = b | 1 << level
            stack = jnp.concatenate([buffer[q, b], buffer[q, p]], axis=0)
            mixed = jnp.dot(matrix(level, n, b, p), stack, preferred_element_type=F32).astype(BF16)
            buffer[q, b] = mixed[:RANK]
            buffer[q, p] = mixed[RANK:]

    def forward_in(level, n, b, p):
        return pair_matrix(win[b, level], win[p, level])

    def forward_out(level, n, b, p):
        return pair_matrix(wout[level, b], wout[level, p])

    def backward_in(level, n, b, p):
        return win_t[level, n]

    def backward_out(level, n, b, p):
        return wout_t[level, n]

    def input_side(q, carry):
        received(xa, 0, q)
        for level in range(LEVELS):
            mix(xa, q, level, forward_in)

        def one(m, c):
            px, pz, pk = relative(m)
            to, r = spread_row(m, q)
            ship(
                xa.at[q, to], xb.at[q, row * 2 + zl],
                send_sem.at[1, q, m], recv_sem.at[1, q], to, r,
            )
            return c

        lax.fori_loop(0, 16, one, 0)
        return carry

    lax.fori_loop(0, 2, input_side, 0)

    for level in range(LEVELS):
        for n, b in enumerate(pairs_of(level)):
            win_t[level, n] = pair_matrix(win[b, level], win[b | 1 << level, level]).T

    def output_side(q, carry):
        received(xb, 1, q)
        for level in range(LEVELS):
            mix(xb, q, level, forward_out)
        for b in range(16):
            twice = jnp.concatenate([xb[q, b], xb[q, b]], axis=0)
            xb[q, b] = jnp.dot(gram[b], twice, preferred_element_type=F32).astype(BF16)
        for level in reversed(range(LEVELS)):
            mix(xb, q, level, backward_out)

        def one(m, c):
            to, r = gather_row(m, q)
            ship(
                xb.at[q, m], xr.at[q, col],
                send_sem.at[2, q, m], recv_sem.at[2, q], to, r,
            )
            return c

        lax.fori_loop(0, 16, one, 0)
        return carry

    lax.fori_loop(0, 2, output_side, 0)

    def input_side_back(q, carry):
        received(xr, 2, q)
        for level in reversed(range(LEVELS)):
            mix(xr, q, level, backward_in)

        def one(m, c):
            px, pz, pk = relative(m)
            to = column(px, pz, pk)
            ship(
                xr.at[q, to], home.at[q, x * 2 + k, zl],
                send_sem.at[3, q, m], recv_sem.at[3, q], to, row,
            )
            return c

        lax.fori_loop(0, 16, one, 0)
        return carry

    lax.fori_loop(0, 2, input_side_back, 0)

    for q in range(2):
        received(home, 3, q)
        outs = [
            pltpu.make_async_copy(
                home.at[q, j, leaf],
                returned.at[leaf, :, pl.ds((q * 8 + j) * LANES, LANES)],
                out_sem.at[q, j, leaf],
            )
            for j in range(8)
            for leaf in range(2)
        ]
        for copy in outs:
            copy.start()
        for copy in outs:
            copy.wait()

    w1.wait_send()
    for copy in w2 + w3 + siblings:
        copy.wait_send()

    def drain(src, send, c, r):
        here = jnp.logical_and(c == col, r == row)

        @pl.when(jnp.logical_not(here))
        def _():
            pltpu.make_async_remote_copy(
                src_ref=src, dst_ref=src, send_sem=send, recv_sem=send,
                device_id={"col": c, "row": r}, device_id_type=MESH,
            ).wait_send()

    def finish(m, carry):
        for q in range(2):
            px, pz, pk = relative(m)
            to = column(px, pz, pk)
            drain(coeffs.at[q, px * 2 + pk, pz], send_sem.at[0, q, m], to, row)
            c, r = spread_row(m, q)
            drain(xa.at[q, c], send_sem.at[1, q, m], c, r)
            c, r = gather_row(m, q)
            drain(xb.at[q, m], send_sem.at[2, q, m], c, r)
            drain(xr.at[q, to], send_sem.at[3, q, m], to, row)
        return carry

    lax.fori_loop(0, 16, finish, 0)


def operator(features, leaf_in, mix_in, mix_out, leaf_out):
    hbm = pl.BlockSpec(memory_space=pltpu.HBM)
    dma = pltpu.SemaphoreType.DMA
    return pl.pallas_call(
        operator_kernel,
        out_shape=jax.ShapeDtypeStruct((2, RANK, features.shape[1]), BF16),
        in_specs=[hbm] * 5,
        out_specs=hbm,
        scratch_shapes=[
            pltpu.VMEM((4, 2 * LEAF, 512), BF16),
            pltpu.VMEM((2 * LEAF, RANK), BF16),
            pltpu.VMEM((2, RANK, LEAF), BF16),
            pltpu.VMEM((16, LEVELS, RANK, 2 * RANK), BF16),
            pltpu.VMEM((LEVELS, 8, 2 * RANK, 2 * RANK), BF16),
            pltpu.VMEM((LEVELS, 16, RANK, 2 * RANK), BF16),
            pltpu.VMEM((LEVELS, 8, 2 * RANK, 2 * RANK), BF16),
            pltpu.VMEM((16 * LEAF, RANK), BF16),
            pltpu.VMEM((16, RANK, 2 * RANK), BF16),
            pltpu.VMEM((2, 8, 2, RANK, LANES), BF16),
            pltpu.VMEM((2, 16, RANK, LANES), BF16),
            pltpu.VMEM((2, 16, RANK, LANES), BF16),
            pltpu.VMEM((2, 16, RANK, LANES), BF16),
            pltpu.VMEM((2, 8, 2, RANK, LANES), BF16),
            dma((8,)), dma((8,)), dma((8,)), dma((1,)), dma((8,)), dma((8,)),
            dma((4, 2, 16)), dma((4, 2)), dma((2, 8, 2)),
        ],
        compiler_params=pltpu.CompilerParams(
            collective_id=0, has_side_effects=True, vmem_limit_bytes=56 << 20
        ),
        name="operator",
    )(features, leaf_in, mix_in, mix_out, leaf_out)


def body(features, leaf_in, mix_in, mix_out, leaf_out):
    returned = operator(features, leaf_in, mix_in, mix_out, leaf_out)
    leaf_rows = leaf_in.reshape(2, LEAF, RANK)
    result = jnp.einsum("bmk,bkr->bmr", leaf_rows, returned, preferred_element_type=F32)
    return result.astype(BF16).reshape(features.shape)


def solution(mesh):
    in_specs = (
        P(("col", "row"), None),
        P(("col", "row"), None),
        P(None, ("col", "row"), None, None),
        P(None, "col", None, None),
        P("col", None),
    )
    out_specs = P(("col", "row"), None)
    return jax.shard_map(body, mesh=mesh, in_specs=in_specs, out_specs=out_specs, check_vma=False)
```

time: 245 us -> 100 us (0.41)
  the two profiles are of different devices: /device:TPU:24 before, /device:TPU:91 now
where the time goes in v1:
time: 100 us; the launch traced here: 99.9 us
  Pallas kernels  92.9 us (93%)
  matrix products  6.96 us (7%)
    pallas_call x1, Pallas kernels, operator(): pl.pallas_call(operator_kernel, out_shape=jax.ShapeDtypeStruct((2, RANK,...  92.9 us
    dot_general x1, matrix products, body(): jnp.einsum('bmk,bkr->bmr', leaf_rows, returned, preferred_element_type=F32)  6.96 us

profile of v1, /device:TPU:91, one launch (start us, length us, event | category | flops | bytes accessed | tf_op | source)
XLA Modules:
  0.0 99.9 jit_solution(14495898330809016573)
XLA Ops:
  0.0 0.0 copy-start
  0.0 92.9 %operator.1 = bf16[2,128,2048]{2,1,0:T(8,128)(2,1)} custom-call(bf16[2048,2048]{1,0:T(8,128)(2,1)} %features.1, bf16[2048,128]{1,0:T(8,128)(2,1)} %leaf_in.1, bf16[4,2,128,256]{3,2,1,0:T(8,128)(2,1)} %mix_in.1, bf16[4,16,128,256]{3,2,1,0:T(8,128)(2,1)} %mix_out.1, bf16[16384,128]{1,0:T(8,128)(2,1)} %leaf_out.1), custom_call_target="tpu_custom_call" | custom-call | tf_op jit(solution)/shard_map/operator/pallas_call | solution.py:351
  92.9 0.0 copy-done
  92.9 7.0 %convolution_convert_fusion = bf16[2,2048,1024]{1,2,0:T(8,128)(2,1)} fusion(bf16[2,1024,128]{2,1,0:T(8,128)(2,1)S(1)} %bitcast.6, bf16[2,128,2048]{2,1,0:T(8,128)(2,1)} %operator.1), kind=kOutput, calls=%fused_computation | convolution fusion | flops 1077936128 | bytes 9961472 | tf_op jit(solution)/shard_map/bmk,bkr->bmr/dot_general | solution.py:384
Async XLA Ops:
  0.0 92.9 %copy-start = (bf16[2048,128]{1,0:T(8,128)(2,1)S(1)}, bf16[2048,128]{1,0:T(8,128)(2,1)}, u32[]{:S(2)}) copy-start(bf16[2048,128]{1,0:T(8,128)(2,1)} %leaf_in.1) | copy-start | bytes 1572868

commit v2 on v1

v2 whole, which is shorter than its diff:
```python
import jax
import jax.numpy as jnp
from jax import lax
from jax.experimental import pallas as pl
from jax.experimental.pallas import tpu as pltpu
from jax.sharding import PartitionSpec as P

LEAF = 1024
RANK = 128
LANES = 128
MESH = pl.DeviceIdType.MESH
F32 = jnp.float32
BF16 = jnp.bfloat16
LEVELS = 4


def pairs_of(bit):
    return [b for b in range(16) if not b >> bit & 1]


def pair_matrix(top, bottom):
    swapped = jnp.concatenate([bottom[:, RANK:], bottom[:, :RANK]], axis=1)
    return jnp.concatenate([top, swapped], axis=0)


def column(x, zl, k):
    return x * 4 + zl * 2 + k


def operator_kernel(
    features, leaf_in, mix_in, mix_out, leaf_out, returned,
    feat, basis, basis_t, win, near_t, far_t, wout, wout_t, lout, gram,
    coeffs, xz, xa, xb, xr, zr,
    load_sem, w_send, w_recv, sib_send, sib_recv, send_sem, recv_sem,
):
    col, row = lax.axis_index("col"), lax.axis_index("row")
    x, zl, k = col // 4, col // 2 % 2, col % 2
    zh, y = row // 4, row % 4
    x_hi, x_lo, y_hi, y_lo = x // 2, x % 2, y // 2, y % 2
    right, left = (x + 1) % 4, (x + 3) % 4

    feat_loads = [
        pltpu.make_async_copy(
            features.at[:, pl.ds(j * 512, 512)], feat.at[j], load_sem.at[j]
        )
        for j in range(4)
    ]
    basis_load = pltpu.make_async_copy(leaf_in, basis, load_sem.at[4])
    wout_load = pltpu.make_async_copy(mix_out, wout, load_sem.at[5])
    lout_load = pltpu.make_async_copy(leaf_out, lout, load_sem.at[6])
    own_load = pltpu.make_async_copy(mix_in.at[:, zl], win.at[col], load_sem.at[7])
    def relative(m):
        px = (x + m + 1) % 4
        pz = (zl + m + m // 4) % 2
        pk = (k + m // 2 + m // 8) % 2
        return px, pz, pk

    def spread_row(m):
        px, pz, pk = relative(m)
        py = (x_lo + px) % 2 * 2 + (x_hi + pk) % 2
        return column(px, pz, pk), k * 4 + py

    def gather_row(m):
        px = (y_lo + k) % 2 * 2 + (y_hi + x) % 2
        return column(px, m % 2, zh), m // 2

    barrier = pltpu.get_barrier_semaphore()

    def greet(m, carry):
        for c, r in (spread_row(m), gather_row(m)):
            pl.semaphore_signal(barrier, device_id={"col": c, "row": r}, device_id_type=MESH)
        return carry

    def near(m):
        pz, pk = (zl + m + 1) % 2, (k + m // 2 + 1) % 2
        return pz, pk, column(x, pz, pk)

    def across(m):
        px = (x + m + 1) % 4
        return px, column(px, zl, k)

    def greet_group(m, carry):
        for c in (near(m)[-1], across(m)[-1]):
            pl.semaphore_signal(barrier, device_id={"col": c, "row": row}, device_id_type=MESH)
        return carry

    for load in [basis_load, *feat_loads[:2]]:
        load.start()
    lax.fori_loop(0, 4, greet_group, 0)
    lax.fori_loop(0, 16, greet, 0)
    pl.semaphore_wait(barrier, 40)

    def ship(src, dst, send, recv, c, r):
        here = jnp.logical_and(c == col, r == row)

        @pl.when(here)
        def _():
            pltpu.make_async_copy(src, dst, recv).start()

        @pl.when(jnp.logical_not(here))
        def _():
            pltpu.make_async_remote_copy(
                src_ref=src, dst_ref=dst, send_sem=send, recv_sem=recv,
                device_id={"col": c, "row": r}, device_id_type=MESH,
            ).start()

    early, late = pl.ds(0, 2), pl.ds(2, 2)

    def weights_to(src, slot, levels, n, recv, c):
        copy = pltpu.make_async_remote_copy(
            src_ref=src, dst_ref=win.at[slot, levels], send_sem=w_send.at[n], recv_sem=recv,
            device_id={"col": c}, device_id_type=MESH,
        )
        copy.start()
        return copy

    def arrived(slot, levels, sem):
        block = win.at[slot, levels]
        pltpu.make_async_copy(block, block, sem).wait()

    siblings = []

    def to_sibling(src, slot, levels):
        n = len(siblings)
        copy = pltpu.make_async_remote_copy(
            src_ref=src, dst_ref=win.at[slot, levels],
            send_sem=sib_send.at[n], recv_sem=sib_recv.at[n],
            device_id={"col": column(x, zl, 1 - k)}, device_id_type=MESH,
        )
        copy.start()
        siblings.append(copy)

    partner = column(x, 1 - zl, k)
    gives = [
        weights_to(mix_in.at[late, 1 - zl], col, late, 0, w_recv.at[0], partner),
        weights_to(mix_in.at[late, zl], col, late, 1, w_recv.at[1 + zl], column(right, zl, k)),
        weights_to(mix_in.at[late, zl], col, late, 2, w_recv.at[3 + zl], column(left, zl, k)),
        weights_to(mix_in.at[early, 1 - zl], col, early, 7, w_recv.at[7], partner),
    ]
    to_sibling(mix_in.at[early, zl], col, early)
    for load in [*feat_loads[2:], own_load]:
        load.start()

    basis_load.wait()
    for leaf in range(2):
        basis_t[leaf] = basis[pl.ds(leaf * LEAF, LEAF), :].T

    def project(q):
        for j in range(2):
            feat_loads[2 * q + j].wait()
            for leaf in range(2):
                block = jnp.dot(
                    basis_t[leaf], feat[2 * q + j, pl.ds(leaf * LEAF, LEAF), :],
                    preferred_element_type=F32,
                ).astype(BF16)
                for i in range(4):
                    coeffs[q, i % 2, leaf, 2 * j + i // 2] = block[:, i * LANES : (i + 1) * LANES]

    def send_coeffs(q):
        def one(m, carry):
            pz, pk, to = near(m)
            ship(
                coeffs.at[q, pk, pz], xz.at[q, zl * 2 + k],
                send_sem.at[0, q, m], recv_sem.at[0, q], to, row,
            )
            return carry

        lax.fori_loop(0, 4, one, 0)

    project(0)
    send_coeffs(0)
    arrived(partner, late, w_recv.at[0])
    block = win.at[partner, late]
    gives += [
        weights_to(block, partner, late, 3, w_recv.at[2 - zl], column(right, zl, k)),
        weights_to(block, partner, late, 4, w_recv.at[4 - zl], column(left, zl, k)),
    ]
    arrived(partner, early, w_recv.at[7])
    to_sibling(win.at[partner, early], partner, early)
    project(1)
    send_coeffs(1)
    lout_load.start()
    wout_load.start()
    to_sibling(mix_in.at[late, zl], col, late)
    to_sibling(win.at[partner, late], partner, late)

    from_left = [column(left, z, k) for z in range(2)]
    from_right = [column(right, z, k) for z in range(2)]
    for slot, sem, n, c in (
        (from_right[0], 3, 5, column(left, zl, k)),
        (from_left[1], 2, 6, column(right, zl, k)),
    ):
        arrived(slot, late, w_recv.at[sem])
        gives.append(weights_to(win.at[slot, late], slot, late, n, w_recv.at[n], c))
        to_sibling(win.at[slot, late], slot, late)
    for slot, sem in ((from_left[0], 1), (from_right[1], 4)):
        arrived(slot, late, w_recv.at[sem])
        to_sibling(win.at[slot, late], slot, late)

    def received(buffer, phase, q):
        pltpu.make_async_copy(buffer.at[q], buffer.at[q], recv_sem.at[phase, q]).wait()

    def mix_near(buffer, q, level, matrix):
        for n, b in enumerate(b for b in range(4) if not b >> level & 1):
            p = b | 1 << level
            for i in (0, 2):
                stack = jnp.concatenate(
                    [
                        jnp.concatenate([buffer[q, c, i], buffer[q, c, i + 1]], axis=1)
                        for c in (b, p)
                    ],
                    axis=0,
                )
                mixed = jnp.dot(
                    matrix(level, n, b, p), stack, preferred_element_type=F32
                ).astype(BF16)
                for c, part in ((b, mixed[:RANK]), (p, mixed[RANK:])):
                    buffer[q, c, i] = part[:, :LANES]
                    buffer[q, c, i + 1] = part[:, LANES:]

    def near_matrix(level, n, b, p):
        return pair_matrix(win[x * 4 + b, level], win[x * 4 + p, level])

    own_load.wait()
    for copy in siblings[:2]:
        copy.wait_recv()

    def near_side(q, carry):
        received(xz, 0, q)
        for level in range(2):
            mix_near(xz, q, level, near_matrix)

        def one(m, c):
            px, to = across(m)
            ship(
                xz.at[q, :, px], xa.at[q, pl.ds(x * 4, 4)],
                send_sem.at[1, q, m], recv_sem.at[1, q], to, row,
            )
            return c

        lax.fori_loop(0, 4, one, 0)
        return carry

    lax.fori_loop(0, 2, near_side, 0)

    far = (x + 2) % 4
    for z in range(2):
        slot = column(far, z, k)
        arrived(slot, late, w_recv.at[5 + z])
        to_sibling(win.at[slot, late], slot, late)

    lout_load.wait()

    def gram_of(i, carry):
        rows = lout[pl.ds(i * LEAF, LEAF), :]
        product = lax.dot_general(rows, rows, (((0,), (0,)), ((), ())), preferred_element_type=F32)
        high = product.astype(BF16)
        low = (product - high.astype(F32)).astype(BF16)
        gram[i] = jnp.concatenate([high, low], axis=1)
        return carry

    lax.fori_loop(0, 16, gram_of, 0)

    wout_load.wait()

    for level in range(LEVELS):
        for n, b in enumerate(pairs_of(level)):
            wout_t[level, n] = pair_matrix(wout[level, b], wout[level, b | 1 << level]).T

    for copy in siblings[2:]:
        copy.wait_recv()

    def mix(buffer, q, level, matrix):
        for n, b in enumerate(pairs_of(level)):
            p = b | 1 << level
            stack = jnp.concatenate([buffer[q, b], buffer[q, p]], axis=0)
            mixed = jnp.dot(matrix(level, n, b, p), stack, preferred_element_type=F32).astype(BF16)
            buffer[q, b] = mixed[:RANK]
            buffer[q, p] = mixed[RANK:]

    def forward_in(level, n, b, p):
        return pair_matrix(win[b, level], win[p, level])

    def forward_out(level, n, b, p):
        return pair_matrix(wout[level, b], wout[level, p])

    def backward_in(level, n, b, p):
        return far_t[level - 2, n]

    def backward_near(level, n, b, p):
        return near_t[level, n]

    def backward_out(level, n, b, p):
        return wout_t[level, n]

    def input_side(q, carry):
        received(xa, 1, q)
        for level in (2, 3):
            mix(xa, q, level, forward_in)

        def one(m, c):
            px, pz, pk = relative(m)
            to, r = spread_row(m)
            ship(
                xa.at[q, to], xb.at[q, row * 2 + zl],
                send_sem.at[2, q, m], recv_sem.at[2, q], to, r,
            )
            return c

        lax.fori_loop(0, 16, one, 0)
        return carry

    lax.fori_loop(0, 2, input_side, 0)

    for level in (2, 3):
        for n, b in enumerate(pairs_of(level)):
            far_t[level - 2, n] = pair_matrix(win[b, level], win[b | 1 << level, level]).T
    for level in range(2):
        for n, b in enumerate(b for b in range(4) if not b >> level & 1):
            near_t[level, n] = near_matrix(level, n, b, b | 1 << level).T

    def output_side(q, carry):
        received(xb, 2, q)
        for level in range(LEVELS):
            mix(xb, q, level, forward_out)
        for b in range(16):
            twice = jnp.concatenate([xb[q, b], xb[q, b]], axis=0)
            xb[q, b] = jnp.dot(gram[b], twice, preferred_element_type=F32).astype(BF16)
        for level in reversed(range(LEVELS)):
            mix(xb, q, level, backward_out)

        def one(m, c):
            to, r = gather_row(m)
            ship(
                xb.at[q, m], xr.at[q, col],
                send_sem.at[3, q, m], recv_sem.at[3, q], to, r,
            )
            return c

        lax.fori_loop(0, 16, one, 0)
        return carry

    lax.fori_loop(0, 2, output_side, 0)

    def input_side_back(q, carry):
        received(xr, 3, q)
        for level in (3, 2):
            mix(xr, q, level, backward_in)

        def one(m, c):
            px, to = across(m)
            ship(
                xr.at[q, pl.ds(px * 4, 4)], zr.at[q, :, x],
                send_sem.at[4, q, m], recv_sem.at[4, q], to, row,
            )
            return c

        lax.fori_loop(0, 4, one, 0)
        return carry

    lax.fori_loop(0, 2, input_side_back, 0)

    def near_side_back(q, carry):
        received(zr, 4, q)
        for level in (1, 0):
            mix_near(zr, q, level, backward_near)

        def one(m, c):
            pz, pk, to = near(m)
            ship(
                zr.at[q, pz * 2 + pk], returned.at[q, k, zl],
                send_sem.at[5, q, m], recv_sem.at[5, q], to, row,
            )
            return c

        lax.fori_loop(0, 4, one, 0)
        return carry

    lax.fori_loop(0, 2, near_side_back, 0)

    for q in range(2):
        received(returned, 5, q)

    for copy in gives + siblings:
        copy.wait_send()

    def drain(src, send, c, r):
        here = jnp.logical_and(c == col, r == row)

        @pl.when(jnp.logical_not(here))
        def _():
            pltpu.make_async_remote_copy(
                src_ref=src, dst_ref=src, send_sem=send, recv_sem=send,
                device_id={"col": c, "row": r}, device_id_type=MESH,
            ).wait_send()

    def finish(m, carry):
        for q in range(2):
            c, r = spread_row(m)
            drain(xa.at[q, c], send_sem.at[2, q, m], c, r)
            c, r = gather_row(m)
            drain(xb.at[q, m], send_sem.at[3, q, m], c, r)
        return carry

    lax.fori_loop(0, 16, finish, 0)

    def finish_group(m, carry):
        for q in range(2):
            pz, pk, to = near(m)
            drain(coeffs.at[q, pk, pz], send_sem.at[0, q, m], to, row)
            drain(zr.at[q, pz * 2 + pk], send_sem.at[5, q, m], to, row)
            px, to = across(m)
            drain(xz.at[q, :, px], send_sem.at[1, q, m], to, row)
            drain(xr.at[q, pl.ds(px * 4, 4)], send_sem.at[4, q, m], to, row)
        return carry

    lax.fori_loop(0, 4, finish_group, 0)


def operator(features, leaf_in, mix_in, mix_out, leaf_out):
    hbm = pl.BlockSpec(memory_space=pltpu.HBM)
    dma = pltpu.SemaphoreType.DMA
    return pl.pallas_call(
        operator_kernel,
        out_shape=jax.ShapeDtypeStruct((2, 2, 2, 4, RANK, LANES), BF16),
        in_specs=[hbm] * 5,
        out_specs=hbm,
        scratch_shapes=[
            pltpu.VMEM((4, 2 * LEAF, 512), BF16),
            pltpu.VMEM((2 * LEAF, RANK), BF16),
            pltpu.VMEM((2, RANK, LEAF), BF16),
            pltpu.VMEM((16, LEVELS, RANK, 2 * RANK), BF16),
            pltpu.VMEM((2, 2, 2 * RANK, 2 * RANK), BF16),
            pltpu.VMEM((2, 8, 2 * RANK, 2 * RANK), BF16),
            pltpu.VMEM((LEVELS, 16, RANK, 2 * RANK), BF16),
            pltpu.VMEM((LEVELS, 8, 2 * RANK, 2 * RANK), BF16),
            pltpu.VMEM((16 * LEAF, RANK), BF16),
            pltpu.VMEM((16, RANK, 2 * RANK), BF16),
            pltpu.VMEM((2, 2, 2, 4, RANK, LANES), BF16),
            pltpu.VMEM((2, 4, 4, RANK, LANES), BF16),
            pltpu.VMEM((2, 16, RANK, LANES), BF16),
            pltpu.VMEM((2, 16, RANK, LANES), BF16),
            pltpu.VMEM((2, 16, RANK, LANES), BF16),
            pltpu.VMEM((2, 4, 4, RANK, LANES), BF16),
            dma((8,)), dma((8,)), dma((8,)), dma((10,)), dma((10,)),
            dma((6, 2, 16)), dma((6, 2)),
        ],
        compiler_params=pltpu.CompilerParams(
            collective_id=0, has_side_effects=True, vmem_limit_bytes=56 << 20
        ),
        name="operator",
    )(features, leaf_in, mix_in, mix_out, leaf_out)


def expand_kernel(rows_in, blocks_in, out, rows, blocks, wide, sems):
    loads = [
        pltpu.make_async_copy(rows_in, rows, sems.at[0]),
        pltpu.make_async_copy(blocks_in, blocks, sems.at[1]),
    ]
    for load in loads:
        load.start()
    for load in loads:
        load.wait()
    stores = []
    for leaf in range(2):
        here = pl.ds(leaf * LEAF, LEAF)
        for part in range(4):
            for i in range(2):
                q, side = part // 2, part % 2 * 2 + i
                columns = jnp.concatenate(
                    [blocks[q, 0, leaf, side], blocks[q, 1, leaf, side]], axis=1
                )
                wide[here, pl.ds(part * 512 + i * 256, 256)] = jnp.dot(
                    rows[here, :], columns, preferred_element_type=F32
                ).astype(BF16)
            tile = pl.ds(part * 512, 512)
            store = pltpu.make_async_copy(
                wide.at[here, tile], out.at[here, tile], sems.at[2 + len(stores)]
            )
            store.start()
            stores.append(store)
    for store in stores:
        store.wait()


def expand(leaf_in, returned, columns):
    hbm = pl.BlockSpec(memory_space=pltpu.HBM)
    return pl.pallas_call(
        expand_kernel,
        out_shape=jax.ShapeDtypeStruct((2 * LEAF, columns), BF16),
        in_specs=[hbm, hbm],
        out_specs=hbm,
        scratch_shapes=[
            pltpu.VMEM((2 * LEAF, RANK), BF16),
            pltpu.VMEM(returned.shape, BF16),
            pltpu.VMEM((2 * LEAF, columns), BF16),
            pltpu.SemaphoreType.DMA((10,)),
        ],
        compiler_params=pltpu.CompilerParams(vmem_limit_bytes=58 << 20),
        name="expand",
    )(leaf_in, returned)


def body(features, leaf_in, mix_in, mix_out, leaf_out):
    returned = operator(features, leaf_in, mix_in, mix_out, leaf_out)
    return expand(leaf_in, returned, features.shape[1])


def solution(mesh):
    in_specs = (
        P(("col", "row"), None),
        P(("col", "row"), None),
        P(None, ("col", "row"), None, None),
        P(None, "col", None, None),
        P("col", None),
    )
    out_specs = P(("col", "row"), None)
    return jax.shard_map(body, mesh=mesh, in_specs=in_specs, out_specs=out_specs, check_vma=False)
```

time: 100 us -> 92.1 us (0.921)
  the two profiles are of different devices: /device:TPU:91 before, /device:TPU:24 now
where the time goes in v2:
time: 92.1 us; the launch traced here: 90.5 us
  Pallas kernels  90.5 us (98%)
    pallas_call x1, Pallas kernels, operator(): pl.pallas_call(operator_kernel, out_shape=jax.ShapeDtypeStruct((2, 2, 2,...  85.3 us
    pallas_call x1, Pallas kernels, expand(): pl.pallas_call(expand_kernel, out_shape=jax.ShapeDtypeStruct((2 * LEAF, c...  5.19 us

profile of v2, /device:TPU:24, one launch (start us, length us, event | category | flops | bytes accessed | tf_op | source)
XLA Modules:
  0.0 90.5 jit_solution(9956785543949130592)
XLA Ops:
  0.0 85.3 %operator.1.blocks_in = bf16[2,2,2,4,128,128]{5,4,3,2,1,0:T(8,128)(2,1)} custom-call(bf16[2048,2048]{1,0:T(8,128)(2,1)} %features.1, bf16[2048,128]{1,0:T(8,128)(2,1)} %rows_in.1, bf16[4,2,128,256]{3,2,1,0:T(8,128)(2,1)} %mix_in.1, bf16[4,16,128,256]{3,2,1,0:T(8,128)(2,1)} %mix_out.1, bf16[16384,128]{1,0:T(8,128)(2,1)} %leaf_out.1), custom_call_target="tpu_custom_call" | custom-call | tf_op jit(solution)/shard_map/operator/pallas_call | solution.py:423
  85.3 5.2 %expand.1 = bf16[2048,2048]{1,0:T(8,128)(2,1)} custom-call(bf16[2048,128]{1,0:T(8,128)(2,1)} %rows_in.1, bf16[2,2,2,4,128,128]{5,4,3,2,1,0:T(8,128)(2,1)} %operator.1.blocks_in), custom_call_target="tpu_custom_call" | custom-call | tf_op jit(solution)/shard_map/expand/pallas_call | solution.py:488

commit v3 on v2

--- a/solution.py
+++ b/solution.py
@@ -62,12 +62,13 @@
 
     def gather_row(m):
         px = (y_lo + k) % 2 * 2 + (y_hi + x) % 2
-        return column(px, m % 2, zh), m // 2
+        pz, py, ph = m % 2, m // 2 % 4, m // 8
+        return column(px, pz, zh), ph * 4 + py, (ph * 4 + py) * 2 + pz
 
     barrier = pltpu.get_barrier_semaphore()
 
     def greet(m, carry):
-        for c, r in (spread_row(m), gather_row(m)):
+        for c, r in (spread_row(m), gather_row(m)[:2]):
             pl.semaphore_signal(barrier, device_id={"col": c, "row": r}, device_id_type=MESH)
         return carry
 
@@ -175,12 +176,12 @@
         weights_to(block, partner, late, 3, w_recv.at[2 - zl], column(right, zl, k)),
         weights_to(block, partner, late, 4, w_recv.at[4 - zl], column(left, zl, k)),
     ]
-    arrived(partner, early, w_recv.at[7])
-    to_sibling(win.at[partner, early], partner, early)
     project(1)
     send_coeffs(1)
     lout_load.start()
     wout_load.start()
+    arrived(partner, early, w_recv.at[7])
+    to_sibling(win.at[partner, early], partner, early)
     to_sibling(mix_in.at[late, zl], col, late)
     to_sibling(win.at[partner, late], partner, late)
 
@@ -241,7 +242,7 @@
         lax.fori_loop(0, 4, one, 0)
         return carry
 
-    lax.fori_loop(0, 2, near_side, 0)
+    near_side(0, 0)
 
     far = (x + 2) % 4
     for z in range(2):
@@ -260,6 +261,7 @@
         return carry
 
     lax.fori_loop(0, 16, gram_of, 0)
+    near_side(1, 0)
 
     wout_load.wait()
 
@@ -330,9 +332,9 @@
             mix(xb, q, level, backward_out)
 
         def one(m, c):
-            to, r = gather_row(m)
+            to, r, b = gather_row(m)
             ship(
-                xb.at[q, m], xr.at[q, col],
+                xb.at[q, b], xr.at[q, col],
                 send_sem.at[3, q, m], recv_sem.at[3, q], to, r,
             )
             return c
@@ -398,8 +400,8 @@
         for q in range(2):
             c, r = spread_row(m)
             drain(xa.at[q, c], send_sem.at[2, q, m], c, r)
-            c, r = gather_row(m)
-            drain(xb.at[q, m], send_sem.at[3, q, m], c, r)
+            c, r, b = gather_row(m)
+            drain(xb.at[q, b], send_sem.at[3, q, m], c, r)
         return carry
 
     lax.fori_loop(0, 16, finish, 0)
@@ -453,18 +455,25 @@
 
 
 def expand_kernel(rows_in, blocks_in, out, rows, blocks, wide, sems):
-    loads = [
-        pltpu.make_async_copy(rows_in, rows, sems.at[0]),
-        pltpu.make_async_copy(blocks_in, blocks, sems.at[1]),
-    ]
-    for load in loads:
-        load.start()
-    for load in loads:
-        load.wait()
+    row_loads, block_loads = [], []
+    for leaf in range(2):
+        half = pl.ds(leaf * LEAF, LEAF)
+        row_loads.append(pltpu.make_async_copy(rows_in.at[half], rows.at[half], sems.at[8 + leaf]))
+        row_loads[-1].start()
+        for q in range(2):
+            block_loads.append(
+                pltpu.make_async_copy(
+                    blocks_in.at[q, :, leaf], blocks.at[q, :, leaf], sems.at[10 + 2 * leaf + q]
+                )
+            )
+            block_loads[-1].start()
     stores = []
     for leaf in range(2):
         here = pl.ds(leaf * LEAF, LEAF)
+        row_loads[leaf].wait()
         for part in range(4):
+            if part % 2 == 0:
+                block_loads[2 * leaf + part // 2].wait()
             for i in range(2):
                 q, side = part // 2, part % 2 * 2 + i
                 columns = jnp.concatenate(
@@ -475,7 +484,7 @@
                 ).astype(BF16)
             tile = pl.ds(part * 512, 512)
             store = pltpu.make_async_copy(
-                wide.at[here, tile], out.at[here, tile], sems.at[2 + len(stores)]
+                wide.at[here, tile], out.at[here, tile], sems.at[len(stores)]
             )
             store.start()
             stores.append(store)
@@ -494,7 +503,7 @@
             pltpu.VMEM((2 * LEAF, RANK), BF16),
             pltpu.VMEM(returned.shape, BF16),
             pltpu.VMEM((2 * LEAF, columns), BF16),
-            pltpu.SemaphoreType.DMA((10,)),
+            pltpu.SemaphoreType.DMA((14,)),
         ],
         compiler_params=pltpu.CompilerParams(vmem_limit_bytes=58 << 20),
         name="expand",

time: 92.1 us -> 90.1 us (0.978); the launches traced: 90.5 us -> 89.9 us
  no operation moved by 1% of the time
where the time goes in v3:
time: 90.1 us; the launch traced here: 89.9 us
  Pallas kernels  89.9 us (100%)
    pallas_call x1, Pallas kernels, operator(): pl.pallas_call(operator_kernel, out_shape=jax.ShapeDtypeStruct((2, 2, 2,...  84.9 us
    pallas_call x1, Pallas kernels, expand(): pl.pallas_call(expand_kernel, out_shape=jax.ShapeDtypeStruct((2 * LEAF, c...  4.96 us

profile of v3, /device:TPU:24, one launch (start us, length us, event | category | flops | bytes accessed | tf_op | source)
XLA Modules:
  0.0 89.9 jit_solution(18413839986583440256)
XLA Ops:
  0.0 84.9 %operator.1.blocks_in = bf16[2,2,2,4,128,128]{5,4,3,2,1,0:T(8,128)(2,1)} custom-call(bf16[2048,2048]{1,0:T(8,128)(2,1)} %features.1, bf16[2048,128]{1,0:T(8,128)(2,1)} %rows_in.1, bf16[4,2,128,256]{3,2,1,0:T(8,128)(2,1)} %mix_in.1, bf16[4,16,128,256]{3,2,1,0:T(8,128)(2,1)} %mix_out.1, bf16[16384,128]{1,0:T(8,128)(2,1)} %leaf_out.1), custom_call_target="tpu_custom_call" | custom-call | tf_op jit(solution)/shard_map/operator/pallas_call | solution.py:425
  84.9 5.0 %expand.1 = bf16[2048,2048]{1,0:T(8,128)(2,1)} custom-call(bf16[2048,128]{1,0:T(8,128)(2,1)} %rows_in.1, bf16[2,2,2,4,128,128]{5,4,3,2,1,0:T(8,128)(2,1)} %operator.1.blocks_in), custom_call_target="tpu_custom_call" | custom-call | tf_op jit(solution)/shard_map/expand/pallas_call | solution.py:497

commit v4 on v3

--- a/solution.py
+++ b/solution.py
@@ -88,7 +88,7 @@
     for load in [basis_load, *feat_loads[:2]]:
         load.start()
     lax.fori_loop(0, 4, greet_group, 0)
-    lax.fori_loop(0, 16, greet, 0)
+    lax.fori_loop(0, 16, greet, 0, unroll=True)
     pl.semaphore_wait(barrier, 40)
 
     def ship(src, dst, send, recv, c, r):
@@ -104,6 +104,16 @@
                 src_ref=src, dst_ref=dst, send_sem=send, recv_sem=recv,
                 device_id={"col": c, "row": r}, device_id_type=MESH,
             ).start()
+
+    def drain(src, send, c, r):
+        here = jnp.logical_and(c == col, r == row)
+
+        @pl.when(jnp.logical_not(here))
+        def _():
+            pltpu.make_async_remote_copy(
+                src_ref=src, dst_ref=src, send_sem=send, recv_sem=send,
+                device_id={"col": c, "row": r}, device_id_type=MESH,
+            ).wait_send()
 
     early, late = pl.ds(0, 2), pl.ds(2, 2)
 
@@ -166,7 +176,7 @@
             )
             return carry
 
-        lax.fori_loop(0, 4, one, 0)
+        lax.fori_loop(0, 4, one, 0, unroll=True)
 
     project(0)
     send_coeffs(0)
@@ -239,7 +249,7 @@
             )
             return c
 
-        lax.fori_loop(0, 4, one, 0)
+        lax.fori_loop(0, 4, one, 0, unroll=True)
         return carry
 
     near_side(0, 0)
@@ -309,7 +319,7 @@
             )
             return c
 
-        lax.fori_loop(0, 16, one, 0)
+        lax.fori_loop(0, 16, one, 0, unroll=True)
         return carry
 
     lax.fori_loop(0, 2, input_side, 0)
@@ -339,10 +349,31 @@
             )
             return c
 
-        lax.fori_loop(0, 16, one, 0)
+        lax.fori_loop(0, 16, one, 0, unroll=True)
         return carry
 
     lax.fori_loop(0, 2, output_side, 0)
+
+    for copy in gives + siblings:
+        copy.wait_send()
+
+    def finish_spread(m, carry):
+        for q in range(2):
+            c, r = spread_row(m)
+            drain(xa.at[q, c], send_sem.at[2, q, m], c, r)
+        return carry
+
+    lax.fori_loop(0, 16, finish_spread, 0)
+
+    def finish_group(m, carry):
+        for q in range(2):
+            pz, pk, to = near(m)
+            drain(coeffs.at[q, pk, pz], send_sem.at[0, q, m], to, row)
+            px, to = across(m)
+            drain(xz.at[q, :, px], send_sem.at[1, q, m], to, row)
+        return carry
+
+    lax.fori_loop(0, 4, finish_group, 0)
 
     def input_side_back(q, carry):
         received(xr, 3, q)
@@ -357,10 +388,18 @@
             )
             return c
 
-        lax.fori_loop(0, 4, one, 0)
+        lax.fori_loop(0, 4, one, 0, unroll=True)
         return carry
 
     lax.fori_loop(0, 2, input_side_back, 0)
+
+    def finish_gather(m, carry):
+        for q in range(2):
+            c, r, b = gather_row(m)
+            drain(xb.at[q, b], send_sem.at[3, q, m], c, r)
+        return carry
+
+    lax.fori_loop(0, 16, finish_gather, 0)
 
     def near_side_back(q, carry):
         received(zr, 4, q)
@@ -375,48 +414,29 @@
             )
             return c
 
-        lax.fori_loop(0, 4, one, 0)
+        lax.fori_loop(0, 4, one, 0, unroll=True)
         return carry
 
     lax.fori_loop(0, 2, near_side_back, 0)
+
+    def finish_across(m, carry):
+        for q in range(2):
+            px, to = across(m)
+            drain(xr.at[q, pl.ds(px * 4, 4)], send_sem.at[4, q, m], to, row)
+        return carry
+
+    lax.fori_loop(0, 4, finish_across, 0)
 
     for q in range(2):
         received(returned, 5, q)
 
-    for copy in gives + siblings:
-        copy.wait_send()
-
-    def drain(src, send, c, r):
-        here = jnp.logical_and(c == col, r == row)
-
-        @pl.when(jnp.logical_not(here))
-        def _():
-            pltpu.make_async_remote_copy(
-                src_ref=src, dst_ref=src, send_sem=send, recv_sem=send,
-                device_id={"col": c, "row": r}, device_id_type=MESH,
-            ).wait_send()
-
-    def finish(m, carry):
-        for q in range(2):
-            c, r = spread_row(m)
-            drain(xa.at[q, c], send_sem.at[2, q, m], c, r)
-            c, r, b = gather_row(m)
-            drain(xb.at[q, b], send_sem.at[3, q, m], c, r)
-        return carry
-
-    lax.fori_loop(0, 16, finish, 0)
-
-    def finish_group(m, carry):
+    def finish_back(m, carry):
         for q in range(2):
             pz, pk, to = near(m)
-            drain(coeffs.at[q, pk, pz], send_sem.at[0, q, m], to, row)
             drain(zr.at[q, pz * 2 + pk], send_sem.at[5, q, m], to, row)
-            px, to = across(m)
-            drain(xz.at[q, :, px], send_sem.at[1, q, m], to, row)
-            drain(xr.at[q, pl.ds(px * 4, 4)], send_sem.at[4, q, m], to, row)
-        return carry
-
-    lax.fori_loop(0, 4, finish_group, 0)
+        return carry
+
+    lax.fori_loop(0, 4, finish_back, 0)
 
 
 def operator(features, leaf_in, mix_in, mix_out, leaf_out):

time: 90.1 us -> 89 us (0.988)
  Pallas kernels: 89.9 us -> 88.7 us
    pallas_call x1, Pallas kernels: 84.9 us -> 83.7 us  [operator(): pl.pallas_call(operator_kernel, out_shape=jax.ShapeDtypeStruct((2, 2, 2,...]
where the time goes in v4:
time: 89 us; the launch traced here: 88.8 us
  Pallas kernels  88.7 us (100%)
    pallas_call x1, Pallas kernels, operator(): pl.pallas_call(operator_kernel, out_shape=jax.ShapeDtypeStruct((2, 2, 2,...  83.7 us
    pallas_call x1, Pallas kernels, expand(): pl.pallas_call(expand_kernel, out_shape=jax.ShapeDtypeStruct((2 * LEAF, c...  4.96 us

profile of v4, /device:TPU:24, one launch (start us, length us, event | category | flops | bytes accessed | tf_op | source)
XLA Modules:
  0.0 88.8 jit_solution(5359554487048984495)
XLA Ops:
  0.0 83.7 %operator.1.blocks_in = bf16[2,2,2,4,128,128]{5,4,3,2,1,0:T(8,128)(2,1)} custom-call(bf16[2048,2048]{1,0:T(8,128)(2,1)} %features.1, bf16[2048,128]{1,0:T(8,128)(2,1)} %rows_in.1, bf16[4,2,128,256]{3,2,1,0:T(8,128)(2,1)} %mix_in.1, bf16[4,16,128,256]{3,2,1,0:T(8,128)(2,1)} %mix_out.1, bf16[16384,128]{1,0:T(8,128)(2,1)} %leaf_out.1), custom_call_target="tpu_custom_call" | custom-call | tf_op jit(solution)/shard_map/operator/pallas_call | solution.py:445
  83.7 5.0 %expand.1 = bf16[2048,2048]{1,0:T(8,128)(2,1)} custom-call(bf16[2048,128]{1,0:T(8,128)(2,1)} %rows_in.1, bf16[2,2,2,4,128,128]{5,4,3,2,1,0:T(8,128)(2,1)} %operator.1.blocks_in), custom_call_target="tpu_custom_call" | custom-call | tf_op jit(solution)/shard_map/expand/pallas_call | solution.py:517

commit v5 on v4

--- a/solution.py
+++ b/solution.py
@@ -274,11 +274,6 @@
     near_side(1, 0)
 
     wout_load.wait()
-
-    for level in range(LEVELS):
-        for n, b in enumerate(pairs_of(level)):
-            wout_t[level, n] = pair_matrix(wout[level, b], wout[level, b | 1 << level]).T
-
     for copy in siblings[2:]:
         copy.wait_recv()
 
@@ -330,6 +325,10 @@
     for level in range(2):
         for n, b in enumerate(b for b in range(4) if not b >> level & 1):
             near_t[level, n] = near_matrix(level, n, b, b | 1 << level).T
+
+    for level in range(LEVELS):
+        for n, b in enumerate(pairs_of(level)):
+            wout_t[level, n] = pair_matrix(wout[level, b], wout[level, b | 1 << level]).T
 
     def output_side(q, carry):
         received(xb, 2, q)

time: 89 us -> 89.5 us (level)
  no operation moved by 1% of the time
where the time goes in v5:
time: 89.5 us; the launch traced here: 88.8 us
  Pallas kernels  88.6 us (99%)
    pallas_call x1, Pallas kernels, operator(): pl.pallas_call(operator_kernel, out_shape=jax.ShapeDtypeStruct((2, 2, 2,...  83.7 us
    pallas_call x1, Pallas kernels, expand(): pl.pallas_call(expand_kernel, out_shape=jax.ShapeDtypeStruct((2 * LEAF, c...  4.96 us

profile of v5, /device:TPU:24, one launch (start us, length us, event | category | flops | bytes accessed | tf_op | source)
XLA Modules:
  0.0 88.8 jit_solution(1830002432663575641)
XLA Ops:
  0.0 83.7 %operator.1.blocks_in = bf16[2,2,2,4,128,128]{5,4,3,2,1,0:T(8,128)(2,1)} custom-call(bf16[2048,2048]{1,0:T(8,128)(2,1)} %features.1, bf16[2048,128]{1,0:T(8,128)(2,1)} %rows_in.1, bf16[4,2,128,256]{3,2,1,0:T(8,128)(2,1)} %mix_in.1, bf16[4,16,128,256]{3,2,1,0:T(8,128)(2,1)} %mix_out.1, bf16[16384,128]{1,0:T(8,128)(2,1)} %leaf_out.1), custom_call_target="tpu_custom_call" | custom-call | tf_op jit(solution)/shard_map/operator/pallas_call | solution.py:444
  83.7 5.0 %expand.1 = bf16[2048,2048]{1,0:T(8,128)(2,1)} custom-call(bf16[2048,128]{1,0:T(8,128)(2,1)} %rows_in.1, bf16[2,2,2,4,128,128]{5,4,3,2,1,0:T(8,128)(2,1)} %operator.1.blocks_in), custom_call_target="tpu_custom_call" | custom-call | tf_op jit(solution)/shard_map/expand/pallas_call | solution.py:516
